TPU v7x, 256 devices: a whole 4x4x8 slice. The times are simulated.
256 devices in a mesh: gen: 8 (over z_lo, core), user: 16 (over x, y), cand: 2 (over z_hi).
Axes of the slice: x: 4, y: 4, z: 8 (z_hi: 2, z_lo: 4; z = z_hi * 4 + z_lo), core: 2. Of those that a mesh axis runs over, the one named last changes fastest.
Arguments:
- states: bfloat16 [16384, 4096], P(('user', 'cand')), may hold values from -6 to 6
- norm_gain: float32 [4096], replicated, may hold values from 0.1 to 1.9
- gate_weight: bfloat16 [4096, 7168], P('user', 'gen'), may hold values from -0.09375 to 0.09375
- up_weight: bfloat16 [4096, 7168], P('user', 'gen'), may hold values from -0.09375 to 0.09375
- down_weight: bfloat16 [7168, 4096], P('gen', 'user'), may hold values from -0.0625 to 0.0625
- proj_weight: bfloat16 [4096, 1024], P('gen'), may hold values from -0.09375 to 0.09375
- private_rows: bfloat16 [32768, 1024], P(('gen', 'user')), may hold values from -6 to 6
- enc_weight: bfloat16 [1024, 1024], replicated, may hold values from -0.1875 to 0.1875
- user_ids: int32 [32768], P(('gen', 'user')), may hold values from 0 to 31
Outputs:
- votes: float32 [16, 2, 128], P(None, 'cand')
Inputs may be any that keep to these rules, and one draw needn't show every extreme that they name: `user_ids`: a user is a pair of a block of 256 rows and a slot; no user has rows in two blocks.
All inputs are finite; a program needn't handle non-finite values.
Results may differ from a plain program's by a relative error of at most 0.0025.
Values may be sent and summed in bfloat16 or wider, within the bound.
No kernel may reach another device: no remote copies, remote signals or barrier semaphores. Data moves between devices by JAX's collectives and lax.ppermute only.
A program may use at most 128 MiB of HBM per device.

v0:
```python
import jax
import jax.numpy as jnp
from jax import lax
from jax.sharding import PartitionSpec as P

STEPS = 4
CAP = 8
USERS_DEV = 32


def unit_rows(matrix):
    return (matrix * lax.rsqrt(jnp.sum(matrix * matrix, axis=1, keepdims=True) + 1e-06)).astype(
        jnp.bfloat16
    )


def project_in(inputs, gate_part, up_part):

    def add_rows(piece):
        return jnp.dot(inputs, piece, preferred_element_type=jnp.float32)

    gate = add_rows(lax.all_gather(gate_part, "user", axis=0, tiled=True))
    up_proj = add_rows(lax.all_gather(up_part, "user", axis=0, tiled=True))
    return (gate, up_proj)


def shards(
    states,
    norm_gain,
    gate_weight,
    up_weight,
    down_weight,
    proj_weight,
    private_rows,
    enc_weight,
    user_ids,
):
    tok_rows, width_model = states.shape
    groups = tok_rows // STEPS
    values = states.astype(jnp.float32)
    normed = (
        values * lax.rsqrt(jnp.mean(values * values, axis=1, keepdims=True) + 1e-05) * norm_gain
    ).astype(jnp.bfloat16)
    gate_part, up_part, down_part = (gate_weight, up_weight, down_weight)
    gate, up_proj = project_in(normed, gate_part, up_part)
    hidden = (jax.nn.silu(gate) * up_proj).astype(jnp.bfloat16)
    mixed = jnp.dot(
        hidden,
        lax.all_gather(down_part, "user", axis=1, tiled=True),
        preferred_element_type=jnp.float32,
    )
    pooled_mlp = jnp.sum(mixed.reshape(-1, STEPS, width_model), axis=1)
    pooled_mlp = lax.psum_scatter(pooled_mlp, "gen", scatter_dimension=1, tiled=True)
    slab_width = pooled_mlp.shape[1]
    own_cols = lax.dynamic_slice_in_dim(values, lax.axis_index("gen") * slab_width, slab_width, 1)
    pooled_in = jnp.sum(own_cols.reshape(groups, STEPS, slab_width), axis=1)
    pooled = ((pooled_in + pooled_mlp) / STEPS).astype(jnp.bfloat16)
    partial_emb = jnp.dot(pooled, proj_weight, preferred_element_type=jnp.float32)
    embedding = lax.psum(partial_emb, "gen")
    candidate = unit_rows(embedding)
    every_cand = lax.all_gather(candidate, "user", axis=0, tiled=True)
    encoded = unit_rows(jnp.dot(private_rows, enc_weight, preferred_element_type=jnp.float32))
    scores = lax.dot_general(
        encoded, every_cand, (((1,), (1,)), ((), ())), preferred_element_type=jnp.float32
    )
    kernel = jnp.exp(scores * 60.0)
    totals = lax.psum(jnp.sum(kernel, axis=1), "cand")
    member = (user_ids[:, None] == jnp.arange(USERS_DEV, dtype=jnp.int32)[None, :]).astype(
        jnp.float32
    )
    counts = jnp.sum(member, axis=0)
    limit = jnp.minimum(1.0, CAP / jnp.maximum(counts, 1.0))
    row_cap = jnp.dot(member, limit, precision=lax.Precision.HIGHEST)
    row_total = private_rows.shape[0] * lax.axis_size("gen") * lax.axis_size("user")
    cand_total = every_cand.shape[0] * lax.axis_size("cand")
    weight_rows = row_cap / totals * (cand_total / row_total)
    partial_votes = jnp.dot(weight_rows, kernel, precision=lax.Precision.HIGHEST)
    votes = lax.psum(partial_votes, ("gen", "user"))
    return votes.reshape(lax.axis_size("user"), 1, groups)


def solution(mesh):
    return jax.shard_map(
        shards,
        mesh=mesh,
        in_specs=(
            P(("user", "cand"), None),
            P(),
            P("user", "gen"),
            P("user", "gen"),
            P("gen", "user"),
            P("gen", None),
            P(("gen", "user"), None),
            P(),
            P(("gen", "user")),
        ),
        out_specs=P(None, "cand", None),
        check_vma=False,
    )
```

profile of v0, /device:TPU:0, one launch (start us, length us, event | category | flops | bytes accessed | tf_op | source)
XLA Modules:
  0.0 810.1 jit_solution(10870717847516051505)
XLA Ops:
  6.5 0.7 all-gather.5.cloned.1.call-update
  7.3 0.0 all-gather.7.cloned.1.call-start
  7.3 0.7 all-gather.7.cloned.1.call-update
  8.1 0.7 all-gather.9.cloned.1.call-update
  8.7 0.0 reduce-scatter.2.cloned.1.call-start
  8.8 3.1 multiply_reduce_fusion
  11.9 70.3 %all-gather.5.cloned.1.call-done = bf16[4096,896]{1,0:T(8,128)(2,1)} async-done(((bf16[256,896]{1,0:T(8,128)(2,1)}), bf16[4096,896]{1,0:T(8,128)(2,1)}) %all-gather.5.cloned.1.call-update) | async-done | bytes 7340048 | tf_op jit(solution)/shard_map/all_gather | solution.py:22
  82.2 10.1 %fusion.1 = f32[512,896]{1,0:T(8,128)} fusion(bf16[4096,896]{1,0:T(8,128)(2,1)} %all-gather.5.cloned.1.call-done, f32[4096]{0:T(1024)S(1)} %copy-done.1, f32[512]{0:T(512)S(1)} %add_rsqrt_fusion, bf16[512,4096]{1,0:T(8,128)(2,1)} %param.9), kind=kOutput, calls=%fused_computation.5 | convolution fusion | flops 3766484992 | bytes 13387776 | tf_op jit(solution)/shard_map/dot_general | solution.py:20
  92.3 63.2 %all-gather.7.cloned.1.call-done = bf16[4096,896]{1,0:T(8,128)(2,1)} async-done(((bf16[256,896]{1,0:T(8,128)(2,1)}), bf16[4096,896]{1,0:T(8,128)(2,1)}) %all-gather.7.cloned.1.call-update) | async-done | bytes 7340048 | tf_op jit(solution)/shard_map/all_gather | solution.py:23
  155.6 79.3 %all-gather.9.cloned.1.call-done = bf16[896,4096]{1,0:T(8,128)(2,1)} async-done(((bf16[896,256]{1,0:T(8,128)(2,1)}), bf16[896,4096]{1,0:T(8,128)(2,1)}) %all-gather.9.cloned.1.call-update) | async-done | bytes 7340048 | tf_op jit(solution)/shard_map/all_gather | solution.py:49
  234.8 17.4 %fusion.2 = f32[512,4096]{1,0:T(8,128)} fusion(bf16[896,4096]{1,0:T(8,128)(2,1)} %all-gather.9.cloned.1.call-done, f32[512,896]{1,0:T(8,128)} %fusion.1, bf16[4096,896]{1,0:T(8,128)(2,1)} %all-gather.7.cloned.1.call-done, f32[4096]{0:T(1024)S(1)} %copy-done.1, f32[512]{0:T(512)S(1)} %add_rsqrt_fusion, bf16[512,4096]{1,0:T(8,128)(2,1)} %param.9), kind=kOutput, calls=%fused_computation.9 | convolution fusion | flops 7527333888 | bytes 29116416 | tf_op jit(solution)/shard_map/dot_general | solution.py:47
  252.2 9.8 %reshape.32 = f32[128,4,4096]{2,1,0:T(4,128)} reshape(f32[512,4096]{1,0:T(8,128)} %fusion.2) | data formatting | bytes 16777216 | tf_op jit(solution)/shard_map/reshape | solution.py:52
  262.0 10.0 %reduce_sum.67 = f32[128,4096]{1,0:T(8,128)} reduce(f32[128,4,4096]{2,1,0:T(4,128)} %reshape.32, f32[]{:T(128)} %constant.15.clone.1), dimensions={1}, to_apply=%region_4.5 | reduce | flops 1572864 | bytes 10485764 | tf_op jit(solution)/shard_map/reduce_sum | solution.py:52
  272.1 0.0 all-reduce.2.cloned.1.call-start
  272.1 6.5 convert_element_type.23
  278.6 1.3 constant_dynamic-slice_fusion
  279.9 1.3 reshape.31
  281.2 1.8 reduce_sum.65
  283.1 29.9 %reduce-scatter.2.cloned.1.call-done = f32[128,512]{1,0:T(8,128)} async-done(((f32[128,4096]{1,0:T(8,128)}), f32[128,512]{1,0:T(8,128)}) %reduce-scatter.2.cloned.1.call-update) | async-done | bytes 262160 | tf_op jit(solution)/shard_map/reduce_scatter | solution.py:53
  313.0 2.4 fusion.4
  315.4 0.3 all-gather.11.cloned.1.call-start
  315.7 70.7 %all-reduce.2.cloned.1.call-done = f32[128,1024]{1,0:T(8,128)} async-done(((f32[128,1024]{1,0:T(8,128)}), f32[128,1024]{1,0:T(8,128)}) %all-reduce.2.cloned.1.call-update) | async-done | bytes 524304 | tf_op jit(solution)/shard_map/psum | solution.py:59
  386.3 1.2 multiply_reduce_fusion.2
  387.5 1.8 multiply_convert_fusion.8
  389.4 0.1 convert_reduce_fusion
  389.5 1.8 multiply_reduce_fusion.1
  391.3 0.1 fusion.6
  391.5 53.5 %all-gather.11.cloned.1.call-done = bf16[2048,1024]{1,0:T(8,128)(2,1)} async-done(((bf16[128,1024]{1,0:T(8,128)(2,1)}), bf16[2048,1024]{1,0:T(8,128)(2,1)}) %all-gather.11.cloned.1.call-update) | async-done | bytes 4194320 | tf_op jit(solution)/shard_map/all_gather | solution.py:61
  445.0 4.9 fusion.16
  449.8 8.8 %psum.22 = f32[256]{0:T(256)S(1)} all-reduce(f32[256]{0:T(256)S(1)} %get-tuple-element.7), channel_id=1, replica_groups=mesh['gen'=8,'user'=16,'cand'=2] {'cand'}, use_global_device_ids=true, to_apply=%region_9.10 | all-reduce | flops 256 | bytes 2048 | tf_op jit(solution)/shard_map/psum | solution.py:67
  458.6 2.7 convolution_bitcast_fusion
  461.3 341.9 %psum.23 = f32[16,1,128]{2,1,0:T(1,128)} all-reduce(f32[16,1,128]{2,1,0:T(1,128)S(1)} %convolution_bitcast_fusion), channel_id=1, replica_groups=mesh['gen'=8,'user'=16,'cand'=2] {'gen','user'}, use_global_device_ids=true, to_apply=%region_10.11 | all-reduce | flops 2048 | bytes 16384 | tf_op jit(solution)/shard_map/psum | solution.py:78
  (15 shorter events, 0.1 us)
Async XLA Ops:
  6.5 383.0 %copy-start = (bf16[1024,1024]{1,0:T(8,128)(2,1)S(1)}, bf16[1024,1024]{1,0:T(8,128)(2,1)}, u32[]{:S(2)}) copy-start(bf16[1024,1024]{1,0:T(8,128)(2,1)} %param.16) | copy-start | bytes 6291460
  6.5 75.7 %copy-start.1 = (f32[4096]{0:T(1024)S(1)}, f32[4096]{0:T(1024)}, u32[]{:S(2)}) copy-start(f32[4096]{0:T(1024)} %param.10) | copy-start | bytes 49156
  6.5 75.7 %all-gather.5.cloned.1.call-start = ((), (), s32[]{:S(2)}) async-start(), calls=%async_computation.1 | async-start | bytes 7798784 | tf_op jit(solution)/shard_map/all_gather | solution.py:22
  7.3 148.3 %all-gather.7.cloned.1.call-start = ((), (), s32[]{:S(2)}) async-start(), calls=%async_computation.2 | async-start | bytes 7798784 | tf_op jit(solution)/shard_map/all_gather | solution.py:23
  8.0 226.8 %all-gather.9.cloned.1.call-start = ((), (), s32[]{:S(2)}) async-start(), calls=%async_computation.3 | async-start | bytes 7798784 | tf_op jit(solution)/shard_map/all_gather | solution.py:49
  8.7 304.2 %reduce-scatter.2.cloned.1.call-start = ((), (), s32[]{:S(2)}) async-start(), calls=%async_computation.4 | async-start | bytes 2359296 | tf_op jit(solution)/shard_map/reduce_scatter | solution.py:53
  272.1 114.3 %all-reduce.2.cloned.1.call-start = ((), (), s32[]{:S(2)}) async-start(), calls=%async_computation.5 | async-start | bytes 1048576 | tf_op jit(solution)/shard_map/psum | solution.py:59
  279.9 109.5 %copy-start.2 = (s32[256]{0:T(256)S(1)}, s32[256]{0:T(256)}, u32[]{:S(2)}) copy-start(s32[256]{0:T(256)} %param.17) | copy-start | bytes 3076
  315.4 129.5 %all-gather.11.cloned.1.call-start = ((), (), s32[]{:S(2)}) async-start(), calls=%async_computation.6 | async-start | bytes 4456448 | tf_op jit(solution)/shard_map/all_gather | solution.py:61
Sparse Core Ops, SparseCore 0:
  9.8 72.3 all-gather.4
  84.7 70.8 all-gather.6
  158.0 76.7 all-gather.8
  272.2 40.7 reduce-scatter.1
  315.5 70.7 all-reduce.1
  389.5 55.4 all-gather.10
where the time goes:
time: 811 us; the launch traced here: 810 us
  waiting for transfers between devices  369 us (45%)
  blocking collectives  351 us (43%)
  matrix products  39.5 us (5%)
  other arithmetic  24.6 us (3%)
  between operations  13.5 us (2%)
  local copies, waits for them, and re-layouts  12.4 us (2%)
    psum x1, blocking collectives, shards(): votes = lax.psum(partial_votes, ('gen', 'user'))  342 us
    all_gather x1, waiting for transfers between devices, shards(): lax.all_gather(down_part, 'user', axis=1, tiled=True)  79.3 us
    psum x1, waiting for transfers between devices, shards(): embedding = lax.psum(partial_emb, 'gen')  70.7 us
    all_gather x1, waiting for transfers between devices, project_in(): gate = add_rows(lax.all_gather(gate_part, 'user', axis=0, tiled=True))  70.3 us
    all_gather x1, waiting for transfers between devices, project_in(): up_proj = add_rows(lax.all_gather(up_part, 'user', axis=0, tiled=True))  63.2 us
    all_gather x1, waiting for transfers between devices, shards(): every_cand = lax.all_gather(candidate, 'user', axis=0, tiled=True)  53.5 us
    reduce_scatter x1, waiting for transfers between devices, shards(): lax.psum_scatter(pooled_mlp, 'gen', scatter_dimension=1, tiled=True)  29.9 us
    dot_general x1, matrix products, shards(): jnp.dot(hidden, lax.all_gather(down_part, 'user', axis=1, tiled=True), pr...  17.4 us
  transfers between devices with their start and end apart: 6, of which 6 were waited for; matrix products, arithmetic and copies ran while one was open for 3% of the time, Pallas kernels for 0%

commit v1 on v0

--- a/solution.py
+++ b/solution.py
@@ -20,7 +20,11 @@
         return jnp.dot(inputs, piece, preferred_element_type=jnp.float32)
 
     gate = add_rows(lax.all_gather(gate_part, "user", axis=0, tiled=True))
-    up_proj = add_rows(lax.all_gather(up_part, "user", axis=0, tiled=True))
+    up_proj = add_rows(
+        jnp.concatenate(
+            lax.all_to_all(jnp.stack([up_part] * lax.axis_size("user")), "user", 0, 0), axis=0
+        )
+    )
     return (gate, up_proj)
 
 

time: 811 us -> 838 us (1.033)
  waiting for transfers between devices: 369 us -> 386 us
    all_gather x1, waiting for transfers between devices: 70.3 us -> 150 us  [project_in(): gate = add_rows(lax.all_gather(gate_part, 'user', axis=0, tiled=True))]
    all_gather x1 -> x0, waiting for transfers between devices: 63.2 us -> none  [project_in(): up_proj = add_rows(lax.all_gather(up_part, 'user', axis=0, tiled=True))]
  transfers between devices with their start and end apart: 6 -> 6, of which waited for: 6 -> 5; matrix products, arithmetic and copies ran while one was open for 3% -> 4% of each run, Pallas kernels for 0% -> 0%
where the time goes in v1:
time: 838 us; the launch traced here: 837 us
  waiting for transfers between devices  386 us (46%)
  blocking collectives  351 us (42%)
  matrix products  39.4 us (5%)
  other arithmetic  24.7 us (3%)
  local copies, waits for them, and re-layouts  17.4 us (2%)
  between operations  13.2 us (2%)
    psum x1, blocking collectives, shards(): votes = lax.psum(partial_votes, ('gen', 'user'))  342 us
    all_gather x1, waiting for transfers between devices, project_in(): gate = add_rows(lax.all_gather(gate_part, 'user', axis=0, tiled=True))  150 us
    all_gather x1, waiting for transfers between devices, shards(): lax.all_gather(down_part, 'user', axis=1, tiled=True)  80.2 us
    psum x1, waiting for transfers between devices, shards(): embedding = lax.psum(partial_emb, 'gen')  70.7 us
    all_gather x1, waiting for transfers between devices, shards(): every_cand = lax.all_gather(candidate, 'user', axis=0, tiled=True)  53.5 us
    reduce_scatter x1, waiting for transfers between devices, shards(): lax.psum_scatter(pooled_mlp, 'gen', scatter_dimension=1, tiled=True)  29.8 us
    dot_general x1, matrix products, shards(): jnp.dot(hidden, lax.all_gather(down_part, 'user', axis=1, tiled=True), pr...  17.3 us
  transfers between devices with their start and end apart: 6, of which 5 were waited for; matrix products, arithmetic and copies ran while one was open for 4% of the time, Pallas kernels for 0%

profile of v1, /device:TPU:0, one launch (start us, length us, event | category | flops | bytes accessed | tf_op | source)
XLA Modules:
  0.0 837.2 jit_solution(5066370205742171028)
XLA Ops:
  6.5 0.7 all-gather.4.cloned.1.call-update
  7.3 0.0 all-gather.6.cloned.1.call-start
  7.3 0.7 all-gather.6.cloned.1.call-update
  8.0 5.0 stack.2
  13.1 5.4 all-to-all-start
  18.4 0.0 reduce-scatter.2.cloned.1.call-start
  18.5 3.1 multiply_reduce_fusion
  21.6 150.2 %all-gather.4.cloned.1.call-done = bf16[4096,896]{1,0:T(8,128)(2,1)} async-done(((bf16[256,896]{1,0:T(8,128)(2,1)}), bf16[4096,896]{1,0:T(8,128)(2,1)}) %all-gather.4.cloned.1.call-update) | async-done | bytes 7340048 | tf_op jit(solution)/shard_map/all_gather | solution.py:22
  171.8 10.1 %fusion.1 = f32[512,896]{1,0:T(8,128)} fusion(bf16[4096,896]{1,0:T(8,128)(2,1)} %all-gather.4.cloned.1.call-done, f32[4096]{0:T(1024)S(1)} %copy-done.1, f32[512]{0:T(512)S(1)} %add_rsqrt_fusion, bf16[512,4096]{1,0:T(8,128)(2,1)} %param.9), kind=kOutput, calls=%fused_computation.5 | convolution fusion | flops 3766484992 | bytes 13387776 | tf_op jit(solution)/shard_map/dot_general | solution.py:20
  181.9 80.2 %all-gather.6.cloned.1.call-done = bf16[896,4096]{1,0:T(8,128)(2,1)} async-done(((bf16[896,256]{1,0:T(8,128)(2,1)}), bf16[896,4096]{1,0:T(8,128)(2,1)}) %all-gather.6.cloned.1.call-update) | async-done | bytes 7340048 | tf_op jit(solution)/shard_map/all_gather | solution.py:53
  262.1 17.3 %fusion.2 = f32[512,4096]{1,0:T(8,128)} fusion(bf16[896,4096]{1,0:T(8,128)(2,1)} %all-gather.6.cloned.1.call-done, f32[512,896]{1,0:T(8,128)} %fusion.1, bf16[4096,896]{1,0:T(8,128)(2,1)} %bitcast.2, f32[4096]{0:T(1024)S(1)} %copy-done.1, f32[512]{0:T(512)S(1)} %add_rsqrt_fusion, bf16[512,4096]{1,0:T(8,128)(2,1)} %param.9), kind=kOutput, calls=%fused_computation.9 | convolution fusion | flops 7527333888 | bytes 29116416 | tf_op jit(solution)/shard_map/dot_general | solution.py:51
  279.4 9.8 %reshape.38 = f32[128,4,4096]{2,1,0:T(4,128)} reshape(f32[512,4096]{1,0:T(8,128)} %fusion.2) | data formatting | bytes 16777216 | tf_op jit(solution)/shard_map/reshape | solution.py:56
  289.2 10.1 %reduce_sum.67 = f32[128,4096]{1,0:T(8,128)} reduce(f32[128,4,4096]{2,1,0:T(4,128)} %reshape.38, f32[]{:T(128)} %constant.15.clone.1), dimensions={1}, to_apply=%region_4.5 | reduce | flops 1572864 | bytes 10485764 | tf_op jit(solution)/shard_map/reduce_sum | solution.py:56
  299.3 0.0 all-reduce.2.cloned.1.call-start
  299.4 6.6 convert_element_type.23
  306.0 1.3 constant_dynamic-slice_fusion
  307.3 1.3 reshape.36
  308.6 1.8 reduce_sum.65
  310.4 29.8 %reduce-scatter.2.cloned.1.call-done = f32[128,512]{1,0:T(8,128)} async-done(((f32[128,4096]{1,0:T(8,128)}), f32[128,512]{1,0:T(8,128)}) %reduce-scatter.2.cloned.1.call-update) | async-done | bytes 262160 | tf_op jit(solution)/shard_map/reduce_scatter | solution.py:57
  340.3 2.4 fusion.4
  342.7 0.3 all-gather.8.cloned.1.call-start
  343.0 70.7 %all-reduce.2.cloned.1.call-done = f32[128,1024]{1,0:T(8,128)} async-done(((f32[128,1024]{1,0:T(8,128)}), f32[128,1024]{1,0:T(8,128)}) %all-reduce.2.cloned.1.call-update) | async-done | bytes 524304 | tf_op jit(solution)/shard_map/psum | solution.py:63
  413.7 1.2 multiply_reduce_fusion.2
  414.9 1.8 multiply_convert_fusion.8
  416.8 0.1 convert_reduce_fusion
  416.9 1.8 multiply_reduce_fusion.1
  418.7 0.1 fusion.6
  418.9 53.5 %all-gather.8.cloned.1.call-done = bf16[2048,1024]{1,0:T(8,128)(2,1)} async-done(((bf16[128,1024]{1,0:T(8,128)(2,1)}), bf16[2048,1024]{1,0:T(8,128)(2,1)}) %all-gather.8.cloned.1.call-update) | async-done | bytes 4194320 | tf_op jit(solution)/shard_map/all_gather | solution.py:65
  472.3 4.9 fusion.16
  477.2 8.8 %psum.22 = f32[256]{0:T(256)S(1)} all-reduce(f32[256]{0:T(256)S(1)} %get-tuple-element.7), channel_id=1, replica_groups=mesh['gen'=8,'user'=16,'cand'=2] {'cand'}, use_global_device_ids=true, to_apply=%region_9.10 | all-reduce | flops 256 | bytes 2048 | tf_op jit(solution)/shard_map/psum | solution.py:71
  486.0 2.7 convolution_bitcast_fusion
  488.7 341.9 %psum.23 = f32[16,1,128]{2,1,0:T(1,128)} all-reduce(f32[16,1,128]{2,1,0:T(1,128)S(1)} %convolution_bitcast_fusion), channel_id=1, replica_groups=mesh['gen'=8,'user'=16,'cand'=2] {'gen','user'}, use_global_device_ids=true, to_apply=%region_10.11 | all-reduce | flops 2048 | bytes 16384 | tf_op jit(solution)/shard_map/psum | solution.py:82
  (15 shorter events, 0.1 us)
Async XLA Ops:
  6.5 410.4 %copy-start = (bf16[1024,1024]{1,0:T(8,128)(2,1)S(1)}, bf16[1024,1024]{1,0:T(8,128)(2,1)}, u32[]{:S(2)}) copy-start(bf16[1024,1024]{1,0:T(8,128)(2,1)} %param.16) | copy-start | bytes 6291460
  6.5 165.2 %all-gather.4.cloned.1.call-start = ((), (), s32[]{:S(2)}) async-start(), calls=%async_computation.2 | async-start | bytes 7798784 | tf_op jit(solution)/shard_map/all_gather | solution.py:22
  7.3 254.8 %all-gather.6.cloned.1.call-start = ((), (), s32[]{:S(2)}) async-start(), calls=%async_computation.3 | async-start | bytes 7798784 | tf_op jit(solution)/shard_map/all_gather | solution.py:53
  13.1 168.8 %all-to-all-start = ((bf16[16,256,896]{2,1,0:T(8,128)(2,1)}), bf16[16,256,896]{2,1,0:T(8,128)(2,1)}, u32[]{:S(2)}, u32[]{:S(2)}) async-start(bf16[16,256,896]{2,1,0:T(8,128)(2,1)} %stack.2), calls=%async_computation | async-start | bytes 14680064 | tf_op jit(solution)/shard_map/all_to_all | solution.py:25
  18.4 153.3 %copy-start.1 = (f32[4096]{0:T(1024)S(1)}, f32[4096]{0:T(1024)}, u32[]{:S(2)}) copy-start(f32[4096]{0:T(1024)} %param.10) | copy-start | bytes 49156
  18.4 321.8 %reduce-scatter.2.cloned.1.call-start = ((), (), s32[]{:S(2)}) async-start(), calls=%async_computation.4 | async-start | bytes 2359296 | tf_op jit(solution)/shard_map/reduce_scatter | solution.py:57
  299.3 114.4 %all-reduce.2.cloned.1.call-start = ((), (), s32[]{:S(2)}) async-start(), calls=%async_computation.5 | async-start | bytes 1048576 | tf_op jit(solution)/shard_map/psum | solution.py:63
  307.3 109.5 %copy-start.2 = (s32[256]{0:T(256)S(1)}, s32[256]{0:T(256)}, u32[]{:S(2)}) copy-start(s32[256]{0:T(256)} %param.17) | copy-start | bytes 3076
  342.7 129.6 %all-gather.8.cloned.1.call-start = ((), (), s32[]{:S(2)}) async-start(), calls=%async_computation.6 | async-start | bytes 4456448 | tf_op jit(solution)/shard_map/all_gather | solution.py:65
Sparse Core Ops, SparseCore 0:
  9.8 161.8 all-gather.3
  174.2 87.8 all-gather.5
  299.4 40.7 reduce-scatter.1
  342.8 70.8 all-reduce.1
  416.9 55.4 all-gather.7
